TPU v7x, 32 devices: a whole 2x2x4 slice. The times are simulated.
32 devices in a mesh: dp: 2 (over x), row: 4 (over y, core), col: 4 (over z).
Axes of the slice: x: 2, y: 2, z: 4, core: 2. Of those that a mesh axis runs over, the one named last changes fastest.
Arguments:
- inputs: bfloat16 [14568, 12, 128], P(('dp', 'row'), 'col'), may hold values from -15 to 15
- mixer_weight: float32 [768, 2304], P('row', 'col'), may hold values from -0.3125 to 0.3125
- mixer_bias: float32 [12, 128], P('col', 'row'), may hold values from -3 to 3
- merge_weight: float32 [768, 768], P(('col', 'row')), may hold values from -0.875 to 0.875
- merge_bias: float32 [12, 64], P('col', 'row'), may hold values from -3 to 3
- expand_weight: float32 [768, 3072], P('row', 'col'), may hold values from -0.21875 to 0.21875
- expand_bias: float32 [12, 256], P('col', 'row'), may hold values from -3 to 3
- reduce_weight: float32 [3072, 768], P(('col', 'row')), may hold values from -0.109375 to 0.109375
- reduce_bias: float32 [12, 64], P('col', 'row'), may hold values from -3 to 3
- first_gain: float32 [12, 64], P('col', 'row'), may hold values from 0.1 to 1.9
- first_shift: float32 [12, 64], P('col', 'row'), may hold values from -3 to 3
- second_gain: float32 [12, 64], P('col', 'row'), may hold values from 0.1 to 1.9
- second_shift: float32 [12, 64], P('col', 'row'), may hold values from -3 to 3
- cotangent: bfloat16 [14568, 12, 128], P(('dp', 'row'), 'col'), may hold values from -6 to 6
Outputs:
- outputs: bfloat16 [14568, 12, 128], P(('dp', 'row'), 'col')
- input_grad: float32 [14568, 12, 128], P(('dp', 'row'), 'col')
- grad_mixer_weight: float32 [768, 2304], P('row', 'col')
- grad_mixer_bias: float32 [12, 128], P('col', 'row')
- grad_merge_weight: float32 [768, 768], P(('col', 'row'))
- grad_merge_bias: float32 [12, 64], P('col', 'row')
- grad_expand_weight: float32 [768, 3072], P('row', 'col')
- grad_expand_bias: float32 [12, 256], P('col', 'row')
- grad_reduce_weight: float32 [3072, 768], P(('col', 'row'))
- grad_reduce_bias: float32 [12, 64], P('col', 'row')
- grad_first_gain: float32 [12, 64], P('col', 'row')
- grad_first_shift: float32 [12, 64], P('col', 'row')
- grad_second_gain: float32 [12, 64], P('col', 'row')
- grad_second_shift: float32 [12, 64], P('col', 'row')
All inputs are finite; a program needn't handle non-finite values.
Results may differ from a plain program's by a relative error of at most 0.012.
The roundings to bfloat16 on the way count: a program that leaves them out, or rounds other values in their place, can miss the bound.
Values may be sent and summed in bfloat16 or wider, within the bound.
A program may use at most 192 MiB of HBM per device.

v0:
```python
import jax
import jax.numpy as jnp
from jax import lax
from jax.sharding import PartitionSpec as P

D = 768
HD = 64
LEN = 1214


EPSILON = 1e-06


def to_rows(values):
    halves = values.shape[0]
    groups = values.shape[1]
    return (
        values.reshape(halves, groups, 2, HD).transpose(0, 2, 1, 3).reshape(2 * halves, groups * HD)
    )


def from_rows(values):
    halves = values.shape[0] // 2
    groups = values.shape[1] // HD
    return (
        values.reshape(halves, 2, groups, HD).transpose(0, 2, 1, 3).reshape(halves, groups, 2 * HD)
    )


def exact_gelu(values):
    return jax.nn.gelu(values, approximate=False)


def inner_rows(left, right):
    return lax.dot_general(
        left, right, (((0,), (0,)), ((), ())), preferred_element_type=jnp.float32
    )


def times_transposed(left, right):
    return lax.dot_general(
        left, right, (((1,), (1,)), ((), ())), preferred_element_type=jnp.float32
    )


def as_vector(values):
    return values.astype(jnp.float32).reshape(-1)


def row_sum(values):
    return lax.psum(values, "col")


def norm_shard(values, gain, shift):
    centre = row_sum(jnp.sum(values, axis=1)) / D
    centered = values - centre[:, None]
    spread = row_sum(jnp.sum(centered * centered, axis=1)) / D
    inverse = lax.rsqrt(spread + EPSILON)
    scaled = centered * inverse[:, None]
    return (scaled * gain + shift, scaled, inverse)


def spread_rows(values):
    return lax.all_gather(values, "col", axis=1, tiled=True)


def gather_grads(values):
    return lax.all_gather(values, "col", axis=1, tiled=True)


def norm_back(partial_rows, scaled, inverse, gain):
    shard = lax.psum_scatter(partial_rows, "col", scatter_dimension=1, tiled=True)
    grad_gain = jnp.sum(shard * scaled, axis=0)
    grad_shift = jnp.sum(shard, axis=0)
    upstream = shard * gain
    first_sum, second_sum = lax.psum(
        (jnp.sum(upstream, axis=1), jnp.sum(upstream * scaled, axis=1)), "col"
    )
    result = inverse[:, None] * (
        upstream - first_sum[:, None] / D - scaled * (second_sum[:, None] / D)
    )
    return (result, grad_gain, grad_shift)


def attend(parts):
    query, keyset, valueset = parts
    scores = times_transposed(query, keyset) * HD ** (-0.5)
    highest = jnp.max(scores, axis=1, keepdims=True)
    weights = jnp.exp(scores - highest)
    totals = jnp.sum(weights, axis=1, keepdims=True)
    chances = (weights / totals).astype(jnp.bfloat16)
    result = jnp.dot(chances, valueset, preferred_element_type=jnp.float32)
    return (result.astype(jnp.bfloat16), (highest + jnp.log(totals))[:, 0])


def attend_back(parts):
    query, keyset, valueset, upstream, logsum = parts
    scale = HD ** (-0.5)
    scores = times_transposed(query, keyset) * scale
    chances = jnp.exp(scores - logsum[:, None])
    grad_chances = times_transposed(upstream, valueset)
    grad_value = inner_rows(chances.astype(jnp.bfloat16), upstream)
    inner = jnp.sum(grad_chances * chances, axis=1, keepdims=True)
    grad_scores = (chances * (grad_chances - inner)).astype(jnp.bfloat16)
    grad_query = jnp.dot(grad_scores, keyset, preferred_element_type=jnp.float32) * scale
    grad_key = inner_rows(grad_scores, query) * scale
    return jnp.stack([grad_query, grad_key, grad_value], axis=1).astype(jnp.bfloat16)


def body(
    inputs,
    mixer_weight,
    mixer_bias,
    merge_weight,
    merge_bias,
    expand_weight,
    expand_bias,
    reduce_weight,
    reduce_bias,
    first_gain,
    first_shift,
    second_gain,
    second_shift,
    cotangent,
):
    (
        mixer_mat,
        mixer_vec,
        merge_mat,
        merge_vec,
        expand_mat,
        expand_vec,
        reduce_mat,
        reduce_vec,
        gain_one,
        shift_one,
        gain_two,
        shift_two,
    ) = (
        lax.all_gather(mixer_weight.astype(jnp.bfloat16), "row", axis=0, tiled=True),
        lax.all_gather(mixer_bias.astype(jnp.bfloat16), "row", axis=1, tiled=True),
        lax.all_gather(merge_weight.astype(jnp.bfloat16), "row", axis=0, tiled=True),
        lax.all_gather(merge_bias.astype(jnp.bfloat16), "row", axis=1, tiled=True),
        lax.all_gather(expand_weight.astype(jnp.bfloat16), "row", axis=0, tiled=True),
        lax.all_gather(expand_bias.astype(jnp.bfloat16), "row", axis=1, tiled=True),
        lax.all_gather(reduce_weight.astype(jnp.bfloat16), "row", axis=0, tiled=True),
        lax.all_gather(reduce_bias.astype(jnp.bfloat16), "row", axis=1, tiled=True),
        lax.all_gather(first_gain.astype(jnp.bfloat16), "row", axis=1, tiled=True),
        lax.all_gather(first_shift.astype(jnp.bfloat16), "row", axis=1, tiled=True),
        lax.all_gather(second_gain.astype(jnp.bfloat16), "row", axis=1, tiled=True),
        lax.all_gather(second_shift.astype(jnp.bfloat16), "row", axis=1, tiled=True),
    )
    rows = to_rows(inputs).astype(jnp.float32)
    cotan_rows = to_rows(cotangent)
    tokens = rows.shape[0]
    width = rows.shape[1]
    clips = tokens // LEN
    local_heads = width // HD
    hidden_width = expand_mat.shape[1]
    gain_first = as_vector(gain_one)
    gain_second = as_vector(gain_two)
    normed_one, scaled_one, inverse_one = norm_shard(rows, gain_first, as_vector(shift_one))
    full_one = spread_rows(normed_one.astype(jnp.bfloat16))
    pairs = mixer_vec.astype(jnp.float32).reshape(local_heads, 2, HD)
    full_bias = jnp.stack([pairs[:, 0], jnp.zeros_like(pairs[:, 0]), pairs[:, 1]], axis=1).reshape(
        -1
    )
    mixed = (jnp.dot(full_one, mixer_mat, preferred_element_type=jnp.float32) + full_bias).astype(
        jnp.bfloat16
    )
    blocks = (
        mixed.reshape(clips, LEN, local_heads, 3, HD)
        .transpose(3, 0, 2, 1, 4)
        .reshape(3, clips * local_heads, LEN, HD)
    )
    head_blocks, logsums = lax.map(attend, (blocks[0], blocks[1], blocks[2]))
    heads = (
        head_blocks.reshape(clips, local_heads, LEN, HD)
        .transpose(0, 2, 1, 3)
        .reshape(tokens, width)
    )
    branch = lax.psum_scatter(
        jnp.dot(heads, merge_mat, preferred_element_type=jnp.float32),
        "col",
        scatter_dimension=1,
        tiled=True,
    )
    state = rows + branch + as_vector(merge_vec)
    normed_two, scaled_two, inverse_two = norm_shard(state, gain_second, as_vector(shift_two))
    full_two = spread_rows(normed_two.astype(jnp.bfloat16))
    hidden = jnp.dot(full_two, expand_mat, preferred_element_type=jnp.float32) + as_vector(
        expand_vec
    )
    active = exact_gelu(hidden).astype(jnp.bfloat16)
    down = lax.psum_scatter(
        jnp.dot(active, reduce_mat, preferred_element_type=jnp.float32).astype(jnp.bfloat16),
        "col",
        scatter_dimension=1,
        tiled=True,
    ).astype(jnp.float32)
    outputs = from_rows((state + down + as_vector(reduce_vec)).astype(jnp.bfloat16))
    cotan_full = gather_grads(cotan_rows)
    grad_reduce_mat = inner_rows(active, cotan_full)
    grad_reduce_vec = jnp.sum(cotan_rows.astype(jnp.float32), axis=0)
    grad_active = times_transposed(cotan_full, reduce_mat)
    gelu_pull = jax.vjp(exact_gelu, hidden)[1]
    grad_hidden = gelu_pull(grad_active)[0].astype(jnp.bfloat16)
    grad_expand_mat = inner_rows(full_two, grad_hidden)
    grad_expand_vec = jnp.sum(grad_hidden.astype(jnp.float32), axis=0)
    back_two, grad_gain_two, grad_shift_two = norm_back(
        times_transposed(grad_hidden, expand_mat), scaled_two, inverse_two, gain_second
    )
    grad_state = cotan_rows.astype(jnp.float32) + back_two
    grad_branch = grad_state.astype(jnp.bfloat16)
    branch_full = gather_grads(grad_branch)
    grad_merge_mat = inner_rows(heads, branch_full)
    grad_merge_vec = jnp.sum(grad_branch.astype(jnp.float32), axis=0)
    grad_heads = times_transposed(branch_full, merge_mat).astype(jnp.bfloat16)
    grad_blocks = (
        grad_heads.reshape(clips, LEN, local_heads, HD)
        .transpose(0, 2, 1, 3)
        .reshape(clips * local_heads, LEN, HD)
    )
    mixed_grads = lax.map(attend_back, (blocks[0], blocks[1], blocks[2], grad_blocks, logsums))
    grad_mixed = (
        mixed_grads.reshape(clips, local_heads, LEN, 3, HD)
        .transpose(0, 2, 1, 3, 4)
        .reshape(tokens, 3 * width)
    )
    grad_mixer_mat = inner_rows(full_one, grad_mixed)
    bias_sums = jnp.sum(grad_mixed.astype(jnp.float32), axis=0).reshape(local_heads, 3, HD)
    grad_mixer_vec = jnp.stack([bias_sums[:, 0], bias_sums[:, 2]], axis=1).reshape(
        local_heads, 2 * HD
    )
    back_one, grad_gain_one, grad_shift_one = norm_back(
        times_transposed(grad_mixed, mixer_mat), scaled_one, inverse_one, gain_first
    )
    input_grad = from_rows(grad_state + back_one)
    (
        part_mixer_mat,
        part_mixer_vec,
        part_merge_mat,
        part_merge_vec,
        part_expand_mat,
        part_expand_vec,
        part_reduce_mat,
        part_reduce_vec,
        part_gain_one,
        part_shift_one,
        part_gain_two,
        part_shift_two,
    ) = (
        lax.psum_scatter(grad_mixer_mat, "row", scatter_dimension=0, tiled=True),
        lax.psum_scatter(grad_mixer_vec, "row", scatter_dimension=1, tiled=True),
        lax.psum_scatter(grad_merge_mat, "row", scatter_dimension=0, tiled=True),
        lax.psum_scatter(
            grad_merge_vec.reshape(local_heads, HD), "row", scatter_dimension=1, tiled=True
        ),
        lax.psum_scatter(grad_expand_mat, "row", scatter_dimension=0, tiled=True),
        lax.psum_scatter(
            grad_expand_vec.reshape(local_heads, hidden_width // local_heads),
            "row",
            scatter_dimension=1,
            tiled=True,
        ),
        lax.psum_scatter(grad_reduce_mat, "row", scatter_dimension=0, tiled=True),
        lax.psum_scatter(
            grad_reduce_vec.reshape(local_heads, HD), "row", scatter_dimension=1, tiled=True
        ),
        lax.psum_scatter(
            grad_gain_one.reshape(local_heads, HD), "row", scatter_dimension=1, tiled=True
        ),
        lax.psum_scatter(
            grad_shift_one.reshape(local_heads, HD), "row", scatter_dimension=1, tiled=True
        ),
        lax.psum_scatter(
            grad_gain_two.reshape(local_heads, HD), "row", scatter_dimension=1, tiled=True
        ),
        lax.psum_scatter(
            grad_shift_two.reshape(local_heads, HD), "row", scatter_dimension=1, tiled=True
        ),
    )
    summed = lax.psum(
        (
            part_mixer_mat,
            part_mixer_vec,
            part_merge_mat,
            part_merge_vec,
            part_expand_mat,
            part_expand_vec,
            part_reduce_mat,
            part_reduce_vec,
            part_gain_one,
            part_shift_one,
            part_gain_two,
            part_shift_two,
        ),
        "dp",
    )
    return (
        outputs,
        input_grad,
        summed[0],
        summed[1],
        summed[2],
        summed[3],
        summed[4],
        summed[5],
        summed[6],
        summed[7],
        summed[8],
        summed[9],
        summed[10],
        summed[11],
    )


def solution(mesh):
    in_specs = (
        P(("dp", "row"), "col", None),
        P("row", "col"),
        P("col", "row"),
        P(("col", "row"), None),
        P("col", "row"),
        P("row", "col"),
        P("col", "row"),
        P(("col", "row"), None),
        P("col", "row"),
        P("col", "row"),
        P("col", "row"),
        P("col", "row"),
        P("col", "row"),
        P(("dp", "row"), "col", None),
    )
    out_specs = (
        P(("dp", "row"), "col", None),
        P(("dp", "row"), "col", None),
        P("row", "col"),
        P("col", "row"),
        P(("col", "row"), None),
        P("col", "row"),
        P("row", "col"),
        P("col", "row"),
        P(("col", "row"), None),
        P("col", "row"),
        P("col", "row"),
        P("col", "row"),
        P("col", "row"),
        P("col", "row"),
    )
    return jax.shard_map(body, mesh=mesh, in_specs=in_specs, out_specs=out_specs, check_vma=False)
```

profile of v0, /device:TPU:0, one launch (start us, length us, event | category | flops | bytes accessed | tf_op | source)
XLA Modules:
  0.0 1910.4 jit_solution(16474213476146647296)
XLA Ops:
  26.0 19.2 %psum.140 = f32[3642]{0:T(1024)S(1)} all-reduce(f32[3642]{0:T(1024)S(1)} %reduce_sum.167), channel_id=1, replica_groups=mesh['dp'=2,'row'=4,'col'=4] {'col'}, use_global_device_ids=true, to_apply=%region_1.0 | all-reduce | flops 3642 | bytes 29136 | tf_op jit(solution)/shard_map/psum | solution.py:51
  106.5 82.4 %all-gather.15.cloned.1.call-done = bf16[3642,768]{0,1:T(8,128)(2,1)} async-done(((bf16[3642,192]{0,1:T(8,128)(2,1)}), bf16[3642,768]{0,1:T(8,128)(2,1)}) %all-gather.15.cloned.1.call-update) | async-done | bytes 5594128 | tf_op jit(solution)/shard_map/all_gather | solution.py:64
  229.9 64.2 %while.22 = (s32[]{:T(128)}, bf16[9,1214,64]{1,2,0:T(8,128)(2,1)}, f32[9,1214]{1,0:T(8,128)}, bf16[9,1214,64]{2,1,0:T(8,128)(2,1)}, bf16[9,1214,64]{2,1,0:T(8,12...) while((s32[]{:T(128)}, bf16[9,1214,64]{1,2,0:T(8,128)(2,1)}, f32[9,1214]{1,0:T(8,128)}, ...), condition=%wide.region_7.8_spmd, body=%wide.region_4.7_spmd.sunk | while | flops 387684832 | bytes 18843696 | solution.py:176
  329.1 173.6 %reduce-scatter.33.cloned.1.call-done = f32[3642,192]{0,1:T(8,128)} async-done(((f32[3642,768]{0,1:T(8,128)}), f32[3642,192]{0,1:T(8,128)}) %reduce-scatter.33.cloned.1.call-update) | async-done | bytes 2797072 | tf_op jit(solution)/shard_map/reduce_scatter | solution.py:182
  505.7 18.5 psum.142
  569.6 76.5 %all-gather.17.cloned.1.call-done = bf16[3642,768]{0,1:T(8,128)(2,1)} async-done(((bf16[3642,192]{0,1:T(8,128)(2,1)}), bf16[3642,768]{0,1:T(8,128)(2,1)}) %all-gather.17.cloned.1.call-update) | async-done | bytes 5594128 | tf_op jit(solution)/shard_map/all_gather | solution.py:64
  663.7 107.1 %all-gather.23.cloned.1.call-done = bf16[3642,768]{0,1:T(8,128)(2,1)} async-done(((bf16[3642,192]{0,1:T(8,128)(2,1)}), bf16[3642,768]{0,1:T(8,128)(2,1)}) %all-gather.23.cloned.1.call-update) | async-done | bytes 5594128 | tf_op jit(solution)/shard_map/all_gather | solution.py:68
  770.8 35.6 %convert_reduce_fusion.1 = (f32[768]{0:T(1024)S(1)}, bf16[3642,768]{1,0:T(8,128)(2,1)S(1)}, f32[3642,768]{1,0:T(8,128)}) fusion(f32[3642,768]{1,0:T(8,128)} %fusion.63, f32[768]{0:T(1024)S(1)} %reshape.245, bf16[3642,768]{0,1:T(8,128)(2,1)} %all-gather.23.cloned.1.call-done, bf16[768,768]{1,0:T(8,128)(2,1)} %all-gather.21.cloned.1.call-done), kind=kOutput, calls=%fused_computation.57 | convolution fusion | flops 4506056704 | bytes 34750464 | tf_op jit(solution)/shard_map/dot_general | solution.py:41
  816.5 190.9 %reduce-scatter.37.cloned.1.call-done = f32[3642,192]{0,1:T(8,128)} async-done(((f32[3642,768]{0,1:T(8,128)}), f32[3642,192]{0,1:T(8,128)}) %reduce-scatter.37.cloned.1.call-update) | async-done | bytes 2797072 | tf_op jit(solution)/shard_map/reduce_scatter | solution.py:72
  1011.0 18.8 all-reduce.1
  1034.8 104.1 %all-gather.25.cloned.1.call-done = bf16[3642,768]{0,1:T(8,128)(2,1)} async-done(((bf16[3642,192]{0,1:T(8,128)(2,1)}), bf16[3642,768]{0,1:T(8,128)(2,1)}) %all-gather.25.cloned.1.call-update) | async-done | bytes 5594128 | tf_op jit(solution)/shard_map/all_gather | solution.py:68
  1150.2 102.2 %while.23 = (s32[]{:T(128)}, bf16[9,1214,3,64]{1,3,2,0:T(8,128)(2,1)}, bf16[9,1214,64]{2,1,0:T(8,128)(2,1)}, bf16[9,1214,64]{2,1,0:T(8,128)(2,1)}, f32[9,1214]{1...) while((s32[]{:T(128)}, ...), condition=%wide.region_21.22_spmd, body=%wide.region_19.21_spmd.sunk | while | flops 956805568 | bytes 48504736 | solution.py:224
  1355.5 118.8 %reduce-scatter.39.cloned.1.call-done = f32[3642,192]{0,1:T(8,128)} async-done(((f32[3642,768]{0,1:T(8,128)}), f32[3642,192]{0,1:T(8,128)}) %reduce-scatter.39.cloned.1.call-update) | async-done | bytes 2797072 | tf_op jit(solution)/shard_map/reduce_scatter | solution.py:72
  1498.6 21.8 %reduce-scatter.53.cloned.1.call-done = f32[64,3]{1,0:T(8,128)} async-done(((f32[256,3]{1,0:T(8,128)}), f32[64,3]{1,0:T(8,128)}) %reduce-scatter.53.cloned.1.call-update) | async-done | bytes 784
  1521.1 21.1 %reduce-scatter.63.cloned.1.call-done = f32[16,3]{1,0:T(8,128)} async-done(((f32[64,3]{1,0:T(8,128)}), f32[16,3]{1,0:T(8,128)}) %reduce-scatter.63.cloned.1.call-update) | async-done | bytes 208
  1543.0 21.2 %reduce-scatter.61.cloned.1.call-done = f32[16,3]{1,0:T(8,128)} async-done(((f32[64,3]{1,0:T(8,128)}), f32[16,3]{1,0:T(8,128)}) %reduce-scatter.61.cloned.1.call-update) | async-done | bytes 208
  1565.0 21.8 %reduce-scatter.51.cloned.1.call-done = f32[16,3]{1,0:T(8,128)} async-done(((f32[64,3]{1,0:T(8,128)}), f32[16,3]{1,0:T(8,128)}) %reduce-scatter.51.cloned.1.call-update) | async-done | bytes 208
  1587.5 21.6 %reduce-scatter.49.cloned.1.call-done = f32[32,3]{1,0:T(8,128)} async-done(((f32[128,3]{1,0:T(8,128)}), f32[32,3]{1,0:T(8,128)}) %reduce-scatter.49.cloned.1.call-update) | async-done | bytes 400
  1610.0 34.6 %reduce-scatter.47.cloned.1.call-done = f32[192,768]{1,0:T(8,128)} async-done(((f32[768,768]{1,0:T(8,128)}), f32[192,768]{1,0:T(8,128)}) %reduce-scatter.47.cloned.1.call-update) | async-done | bytes 589840 | tf_op jit(solution)/shard_map/reduce_scatter | solution.py:266
  1644.6 35.8 %reduce-scatter.45.cloned.1.call-done = f32[192,768]{1,0:T(8,128)} async-done(((f32[768,768]{1,0:T(8,128)}), f32[192,768]{1,0:T(8,128)}) %reduce-scatter.45.cloned.1.call-update) | async-done | bytes 589840 | tf_op jit(solution)/shard_map/reduce_scatter | solution.py:259
  1680.4 25.2 %reduce-scatter.43.cloned.1.call-done = f32[48,768]{1,0:T(8,128)} async-done(((f32[192,768]{1,0:T(8,128)}), f32[48,768]{1,0:T(8,128)}) %reduce-scatter.43.cloned.1.call-update) | async-done | bytes 147472 | tf_op jit(solution)/shard_map/reduce_scatter | solution.py:255
  1705.6 32.8 %reduce-scatter.41.cloned.1.call-done = f32[192,576]{1,0:T(8,128)} async-done(((f32[768,576]{1,0:T(8,128)}), f32[192,576]{1,0:T(8,128)}) %reduce-scatter.41.cloned.1.call-update) | async-done | bytes 442384 | tf_op jit(solution)/shard_map/reduce_scatter | solution.py:253
  1738.4 20.2 %all-reduce = (f32[3642]{0:T(1024)S(1)}, f32[3642]{0:T(1024)S(1)}) all-reduce(f32[3642]{0:T(1024)S(1)} %get-tuple-element.185, f32[3642]{0:T(1024)S(1)} %get-tuple-element.186), channel_id=1, replica_groups=mesh['dp'=2,'row'=4,'col'=4] {'col'}, use_global_device_ids=true, to_apply=%region_26.27 | all-reduce | flops 7284 | bytes 58272 | tf_op jit(solution)/shard_map/psum | solution.py:76
  1758.7 83.7 %reduce-scatter.35.cloned.1.call-done = bf16[3642,192]{0,1:T(8,128)(2,1)} async-done(((bf16[3642,768]{0,1:T(8,128)(2,1)}), bf16[3642,192]{0,1:T(8,128)(2,1)}) %reduce-scatter.35.cloned.1.call-update) | async-done | bytes 1398544 | tf_op jit(solution)/shard_map/reduce_scatter | solution.py:195
  (399 shorter events, 608.5 us)
Async XLA Ops:
  8.0 180.9 %all-gather.15.cloned.1.call-start = ((), (), s32[]{:S(2)}) async-start(), calls=%async_computation.16 | async-start | bytes 7127040 | tf_op jit(solution)/shard_map/all_gather | solution.py:64
  84.6 418.0 %reduce-scatter.33.cloned.1.call-start = ((), (), s32[]{:S(2)}) async-start(), calls=%async_computation.17 | async-start | bytes 14254080 | tf_op jit(solution)/shard_map/reduce_scatter | solution.py:182
  311.4 258.2 %all-gather.19.cloned.1.call-start = ((), (), s32[]{:S(2)}) async-start(), calls=%async_computation.19 | async-start | bytes 1474560 | tf_op jit(solution)/shard_map/all_gather | solution.py:144
  313.2 332.9 %all-gather.17.cloned.1.call-start = ((), (), s32[]{:S(2)}) async-start(), calls=%async_computation.18 | async-start | bytes 7127040 | tf_op jit(solution)/shard_map/all_gather | solution.py:64
  323.8 706.2 %copy-start.23 = (f32[192]{0:T(256)}, f32[192]{0:T(256)S(1)}, u32[]{:S(2)}) copy-start(f32[192]{0:T(256)S(1)} %reshape.243) | copy-start | bytes 2308
  541.8 121.9 %all-gather.21.cloned.1.call-start = ((), (), s32[]{:S(2)}) async-start(), calls=%async_computation.20 | async-start | bytes 1474560 | tf_op jit(solution)/shard_map/all_gather | solution.py:146
  543.7 227.1 %all-gather.23.cloned.1.call-start = ((), (), s32[]{:S(2)}) async-start(), calls=%async_computation.22 | async-start | bytes 7127040 | tf_op jit(solution)/shard_map/all_gather | solution.py:68
  564.3 443.1 %reduce-scatter.37.cloned.1.call-start = ((), (), s32[]{:S(2)}) async-start(), calls=%async_computation.23 | async-start | bytes 14254080 | tf_op jit(solution)/shard_map/reduce_scatter | solution.py:72
  816.3 322.6 %all-gather.25.cloned.1.call-start = ((), (), s32[]{:S(2)}) async-start(), calls=%async_computation.24 | async-start | bytes 7127040 | tf_op jit(solution)/shard_map/all_gather | solution.py:68
  1034.7 439.6 %reduce-scatter.39.cloned.1.call-start = ((), (), s32[]{:S(2)}) async-start(), calls=%async_computation.25 | async-start | bytes 14254080 | tf_op jit(solution)/shard_map/reduce_scatter | solution.py:72
  1283.0 214.8 %reduce-scatter.55.cloned.1.call-start = ((), (), s32[]{:S(2)}) async-start(), calls=%async_computation.33 | async-start | bytes 40960
  1285.4 234.9 %reduce-scatter.53.cloned.1.call-start = ((), (), s32[]{:S(2)}) async-start(), calls=%async_computation.32 | async-start | bytes 163840
  1286.3 256.0 %reduce-scatter.63.cloned.1.call-start = ((), (), s32[]{:S(2)}) async-start(), calls=%async_computation.37 | async-start | bytes 40960
  1287.2 277.1 %reduce-scatter.61.cloned.1.call-start = ((), (), s32[]{:S(2)}) async-start(), calls=%async_computation.36 | async-start | bytes 40960
  1288.0 298.7 %reduce-scatter.51.cloned.1.call-start = ((), (), s32[]{:S(2)}) async-start(), calls=%async_computation.31 | async-start | bytes 40960
  1300.0 309.2 %reduce-scatter.49.cloned.1.call-start = ((), (), s32[]{:S(2)}) async-start(), calls=%async_computation.30 | async-start | bytes 81920
  1309.1 335.5 %reduce-scatter.47.cloned.1.call-start = ((), (), s32[]{:S(2)}) async-start(), calls=%async_computation.29 | async-start | bytes 2949120 | tf_op jit(solution)/shard_map/reduce_scatter | solution.py:266
  1320.0 360.4 %reduce-scatter.45.cloned.1.call-start = ((), (), s32[]{:S(2)}) async-start(), calls=%async_computation.28 | async-start | bytes 2949120 | tf_op jit(solution)/shard_map/reduce_scatter | solution.py:259
  1330.6 375.0 %reduce-scatter.43.cloned.1.call-start = ((), (), s32[]{:S(2)}) async-start(), calls=%async_computation.27 | async-start | bytes 737280 | tf_op jit(solution)/shard_map/reduce_scatter | solution.py:255
  1335.9 402.5 %reduce-scatter.41.cloned.1.call-start = ((), (), s32[]{:S(2)}) async-start(), calls=%async_computation.26 | async-start | bytes 2457600 | tf_op jit(solution)/shard_map/reduce_scatter | solution.py:253
  1346.2 496.2 %reduce-scatter.35.cloned.1.call-start = ((), (), s32[]{:S(2)}) async-start(), calls=%async_computation.21 | async-start | bytes 7127040 | tf_op jit(solution)/shard_map/reduce_scatter | solution.py:195
  1355.5 525.1 %reduce-scatter.59.cloned.1.call-start = ((), (), s32[]{:S(2)}) async-start(), calls=%async_computation.35 | async-start | bytes 40960
  1479.6 406.7 %reduce-scatter.57.cloned.1.call-start = ((), (), s32[]{:S(2)}) async-start(), calls=%async_computation.34 | async-start | bytes 40960
  1485.6 410.2 %all-reduce.6.cloned.1.call-start = ((), (), s32[]{:S(2)}) async-start(), calls=%async_computation.38 | async-start | bytes 3637248 | tf_op jit(solution)/shard_map/psum | solution.py:283
  (35 other events, 5198.6 us)
Sparse Core Ops, SparseCore 0:
  84.8 104.1 all-gather.14
  311.5 191.0 reduce-scatter.32
  1034.8 104.0 all-gather.24
  1283.1 191.1 reduce-scatter.38
  1477.1 20.6 reduce-scatter.54
  1500.6 19.6 reduce-scatter.52
  1522.7 19.5 reduce-scatter.62
  1544.7 19.5 reduce-scatter.60
  1567.2 19.5 reduce-scatter.50
  1589.6 19.5 reduce-scatter.48
  1611.7 32.8 reduce-scatter.46
  1647.5 32.8 reduce-scatter.44
  1683.5 22.0 reduce-scatter.42
  1708.0 30.3 reduce-scatter.40
  1740.6 101.7 reduce-scatter.34
  1844.6 19.8 reduce-scatter.58
  1866.7 19.5 reduce-scatter.56
Sparse Core Ops, SparseCore 1:
  314.0 15.6 all-gather.18
  541.9 104.1 all-gather.16
  648.1 15.5 all-gather.20
  665.3 105.4 all-gather.22
  816.4 191.0 reduce-scatter.36
  1738.5 56.7 all-reduce.5
where the time goes:
time: 1920 us; the launch traced here: 1910 us
  waiting for transfers between devices  1200 us (62%)
  matrix products  251 us (13%)
  local copies, waits for them, and re-layouts  193 us (10%)
  blocking collectives  175 us (9%)
  other arithmetic  76.7 us (4%)
    reduce_scatter x2, waiting for transfers between devices, norm_back(): lax.psum_scatter(partial_rows, 'col', scatter_dimension=1, tiled=True)  310 us
    all_gather x2, waiting for transfers between devices, gather_grads(): return lax.all_gather(values, 'col', axis=1, tiled=True)  211 us
    reduce_scatter x1, waiting for transfers between devices, body(): lax.psum_scatter(jnp.dot(heads, merge_mat, preferred_element_type=jnp.flo...  174 us
    all_gather x2, waiting for transfers between devices, spread_rows(): return lax.all_gather(values, 'col', axis=1, tiled=True)  159 us
    unnamed x31, waiting for transfers between devices  125 us
    dot_general x31, matrix products, times_transposed(): lax.dot_general(left, right, (((1,), (1,)), ((), ())), preferred_element_...  111 us
    reduce_scatter x1, waiting for transfers between devices, body(): lax.psum_scatter(jnp.dot(active, reduce_mat, preferred_element_type=jnp.f...  83.7 us
    psum x4, blocking collectives, row_sum(): return lax.psum(values, 'col')  68.8 us
  transfers between devices with their start and end apart: 23, of which 20 were waited for; matrix products, arithmetic and copies ran while one was open for 8% of the time, Pallas kernels for 0%

commit v1 on v0

v1 whole, which is shorter than its diff:
```python
import functools

import jax
import jax.numpy as jnp
from jax import lax
from jax.experimental import pallas as pl
from jax.experimental.pallas import tpu as pltpu
from jax.sharding import PartitionSpec as P

D = 768
HD = 64
LEN = 1214
EPSILON = 1e-06
PAIRS = LEN // 2
TILE = 152
ROWS = 2 * TILE
KEYS = 4 * ROWS
WIDE = 640
BLOCK = 304
NT = (((1,), (1,)), ((), ()))
TN = (((0,), (0,)), ((), ()))
NN = (((1,), (0,)), ((), ()))
f32 = jnp.float32
bf16 = jnp.bfloat16
PLANE = ("row", "col")
BLOCKS = ("col", "row")


def dot(left, right, dims=NN):
    return lax.dot_general(left, right, dims, preferred_element_type=f32)


HEADS = ((0, 1, 2, 0, 0), (0, 1, 2, 1, 1), (3, 4, 3, 0, 1))
ORDER = ((0, 0), (1, 0), (0, 1), (1, 1), (0, 2), (1, 2), (2, 0), (2, 2), (2, 1))


def widen(values):
    pieces = [values[..., (3 * h + s) * HD : (3 * h + s + 1) * HD] for h, s in ORDER]
    pieces.append(jnp.zeros_like(pieces[0]))
    return jnp.concatenate(pieces, axis=-1)


def narrow(values):
    place = {pair: at for at, pair in enumerate(ORDER)}
    pieces = []
    for h in range(3):
        for s in range(3):
            at = place[(h, s)]
            pieces.append(values[..., at * HD : (at + 1) * HD])
    return jnp.concatenate(pieces, axis=-1)


def key_bias():
    index = lax.broadcasted_iota(jnp.int32, (1, KEYS), 1)
    padded = (index == KEYS - 1 - TILE) | (index == KEYS - 1)
    return jnp.where(padded, -1e30, 0.0).astype(f32)


def tile(ref, at):
    return ref[0, :, 128 * at : 128 * at + 128]


def attend_kernel(mixed_ref, out_ref, sum_ref):
    bias = key_bias()
    lane = lax.broadcasted_iota(jnp.int32, (1, 128), 1)
    low = lane < HD

    def block(step, carry):
        rows = pl.ds(pl.multiple_of(step * BLOCK, 8), BLOCK)
        outs = []
        sums = []
        for qt, kt, vt, qh, vh in HEADS:
            query = mixed_ref[0, rows, 128 * qt : 128 * qt + 128]
            query = jnp.where(low == (qh == 0), query, jnp.zeros_like(query))
            query = query * jnp.asarray(0.125, bf16)
            scores = dot(query, tile(mixed_ref, kt), NT) + bias
            highest = jnp.max(scores, axis=1, keepdims=True)
            weights = jnp.exp(scores - highest)
            total = jnp.sum(weights, axis=1, keepdims=True)
            outs.append(dot(weights.astype(bf16), tile(mixed_ref, vt)) * (1.0 / total))
            sums.append(highest + jnp.log(total))
        out_ref[0, rows, 0:128] = jnp.where(low, outs[0], outs[1]).astype(bf16)
        out_ref[0, rows, 128:256] = jnp.where(low, 0.0, outs[2]).astype(bf16)
        sum_ref[0, rows, :] = jnp.where(lane == 0, sums[0], jnp.where(lane == 1, sums[1], sums[2]))
        return carry

    lax.fori_loop(0, KEYS // BLOCK, block, 0)


def attend(mixed):
    slots = mixed.shape[0]
    return pl.pallas_call(
        attend_kernel,
        grid=(slots,),
        in_specs=[pl.BlockSpec((1, KEYS, WIDE), lambda i: (i, 0, 0))],
        out_specs=[
            pl.BlockSpec((1, KEYS, 256), lambda i: (i, 0, 0)),
            pl.BlockSpec((1, KEYS, 128), lambda i: (i, 0, 0)),
        ],
        out_shape=[
            jax.ShapeDtypeStruct((slots, KEYS, 256), bf16),
            jax.ShapeDtypeStruct((slots, KEYS, 128), f32),
        ],
        cost_estimate=pl.CostEstimate(
            flops=12 * slots * KEYS * KEYS * 128,
            bytes_accessed=slots * KEYS * 2 * (WIDE + 512),
            transcendentals=3 * slots * KEYS * KEYS,
        ),
        name="attend",
    )(mixed)


def attend_back_kernel(mixed_ref, grad_ref, sum_ref, out_ref, key_sum, value_sum):
    bias = key_bias()
    lane = lax.broadcasted_iota(jnp.int32, (1, 128), 1)
    low = lane < HD
    key_sum[...] = jnp.zeros_like(key_sum)
    value_sum[...] = jnp.zeros_like(value_sum)

    def block(step, carry):
        rows = pl.ds(pl.multiple_of(step * BLOCK, 8), BLOCK)
        sums = sum_ref[0, rows, :]
        queries = []
        for head, (qt, kt, vt, qh, vh) in enumerate(HEADS):
            query = mixed_ref[0, rows, 128 * qt : 128 * qt + 128]
            query = jnp.where(low == (qh == 0), query, jnp.zeros_like(query))
            query = query * jnp.asarray(0.125, bf16)
            at = head // 2
            grad = grad_ref[0, rows, 128 * at : 128 * at + 128]
            grad = jnp.where(low == (vh == 0), grad, jnp.zeros_like(grad))
            scores = dot(query, tile(mixed_ref, kt), NT) + bias
            chances = jnp.exp(scores - sums[:, head : head + 1])
            grad_chances = dot(grad, tile(mixed_ref, vt), NT)
            inner = jnp.sum(grad_chances * chances, axis=1, keepdims=True)
            grad_scores = (chances * (grad_chances - inner)).astype(bf16)
            value_sum[at] += dot(chances.astype(bf16), grad, TN)
            key_sum[at] += dot(grad_scores, query, TN)
            queries.append(dot(grad_scores, tile(mixed_ref, kt)) * 0.125)
        out_ref[0, rows, 0:128] = jnp.where(low, queries[0], queries[1]).astype(bf16)
        out_ref[0, rows, 384:512] = jnp.where(low, queries[2], 0.0).astype(bf16)
        return carry

    lax.fori_loop(0, KEYS // BLOCK, block, 0)
    out_ref[0, :, 128:256] = key_sum[0].astype(bf16)
    out_ref[0, :, 256:384] = value_sum[0].astype(bf16)
    out_ref[0, :, 384:512] = jnp.where(low, out_ref[0, :, 384:512], value_sum[1].astype(bf16))
    out_ref[0, :, 512:640] = key_sum[1].astype(bf16)


def attend_back(mixed, grads, sums):
    slots = mixed.shape[0]
    return pl.pallas_call(
        attend_back_kernel,
        grid=(slots,),
        in_specs=[
            pl.BlockSpec((1, KEYS, WIDE), lambda i: (i, 0, 0)),
            pl.BlockSpec((1, KEYS, 256), lambda i: (i, 0, 0)),
            pl.BlockSpec((1, KEYS, 128), lambda i: (i, 0, 0)),
        ],
        out_specs=pl.BlockSpec((1, KEYS, WIDE), lambda i: (i, 0, 0)),
        out_shape=jax.ShapeDtypeStruct((slots, KEYS, WIDE), bf16),
        scratch_shapes=[pltpu.VMEM((2, KEYS, 128), f32), pltpu.VMEM((2, KEYS, 128), f32)],
        cost_estimate=pl.CostEstimate(
            flops=30 * slots * KEYS * KEYS * 128,
            bytes_accessed=slots * KEYS * 2 * (2 * WIDE + 512),
            transcendentals=3 * slots * KEYS * KEYS,
        ),
        name="attend_back",
    )(mixed, grads, sums)


def plane_index(row, col):
    return 4 * row + col


def spread_pairs(step):
    pairs = []
    for half in range(2):
        for bit in range(2):
            for col in range(4):
                member = col ^ step
                pairs.append(
                    (
                        plane_index(2 * half + bit, col),
                        plane_index(2 * half + member // 2, 2 * bit + member % 2),
                    )
                )
    return pairs


def take(values, index):
    return lax.dynamic_index_in_dim(values, index, 0, keepdims=False)


def to_members(values, col, member):
    width = values.shape[1] * values.shape[2]
    clips = values.reshape(-1, PAIRS, width)
    last = jnp.pad(clips[:, 3 * TILE :], ((0, 0), (0, 4 * TILE - PAIRS), (0, 0)))
    blocks = jnp.concatenate([clips[:, : 3 * TILE], last.reshape(1, 3 * TILE, width)])
    got = jnp.stack(
        [lax.ppermute(take(blocks, col ^ step), PLANE, spread_pairs(step)) for step in range(4)]
    )
    whole = jnp.concatenate([take(got, source ^ member) for source in range(4)], axis=1)
    heads = 4 * values.shape[1]
    return (
        whole.reshape(3, TILE, heads, 2, HD)
        .transpose(0, 3, 1, 2, 4)
        .reshape(3 * ROWS, heads * HD)
    )


def from_members(values, col, member):
    heads = values.shape[1] // HD
    width = values.shape[1] * 2 // 4
    whole = values.reshape(3, 2, TILE, heads, HD).transpose(0, 2, 3, 1, 4)
    parts = whole.reshape(3 * TILE, 4, width).transpose(1, 0, 2)
    got = jnp.stack(
        [
            lax.ppermute(
                take(parts, member ^ step),
                PLANE,
                [(target, source) for source, target in spread_pairs(step)],
            )
            for step in range(4)
        ]
    )
    blocks = jnp.stack([take(got, col ^ other) for other in range(4)])
    last = blocks[3].reshape(3, TILE, width)[:, : PAIRS - 3 * TILE]
    clips = jnp.concatenate([blocks[:3], last], axis=1)
    return clips.reshape(3 * PAIRS, width // 128, 128)


def swap_pairs(member):
    pairs = []
    for half in range(2):
        for pair in range(2):
            one = plane_index(2 * half + member // 2, 2 * pair + member % 2)
            other = plane_index(2 * half + 1, 2 * pair + 1)
            pairs += [(one, other), (other, one)]
    return pairs


def to_slots(values, last):
    got = [
        lax.ppermute(jnp.where(last, values[:3, at], values[3]), PLANE, swap_pairs(at))
        for at in range(3)
    ]
    mine = got[0] + got[1] + got[2]
    head = jnp.where(last, jnp.stack(got), values[:3])
    tail = jnp.where(last, values[3], mine)
    return jnp.concatenate([head, tail[:, None]], axis=1)


def from_slots(values, last):
    got = [
        lax.ppermute(jnp.where(last, values[at, :3], values[:, 3]), PLANE, swap_pairs(at))
        for at in range(3)
    ]
    mine = got[0] + got[1] + got[2]
    head = jnp.where(last, jnp.stack(got, axis=1), values[:, :3])
    tail = jnp.where(last, values[:, 3], mine)
    return jnp.concatenate([head, tail[None]])


def norm(values, gain, shift):
    centre = jnp.mean(values, axis=1, keepdims=True)
    centered = values - centre
    spread = jnp.mean(centered * centered, axis=1, keepdims=True)
    inverse = lax.rsqrt(spread + EPSILON)
    scaled = centered * inverse
    return (scaled * gain + shift, scaled, inverse)


def norm_back(grads, scaled, inverse, gain):
    upstream = grads * gain
    first = jnp.mean(upstream, axis=1, keepdims=True)
    second = jnp.mean(upstream * scaled, axis=1, keepdims=True)
    result = inverse * (upstream - first - scaled * second)
    return (result, jnp.sum(grads * scaled, axis=0), jnp.sum(grads, axis=0))


def many(left, right, left_dims, right_dims, left_batch=(), right_batch=()):
    return lax.dot_general(
        left,
        right,
        ((left_dims, right_dims), (left_batch, right_batch)),
        preferred_element_type=f32,
    )


def gelu_parts(values):
    chance = 0.5 * (1.0 + lax.erf(values * (0.5**0.5)))
    density = jnp.exp(-0.5 * values * values) * (0.5 / jnp.pi) ** 0.5
    return (values * chance, chance + values * density)


def body(
    inputs,
    mixer_weight,
    mixer_bias,
    merge_weight,
    merge_bias,
    expand_weight,
    expand_bias,
    reduce_weight,
    reduce_bias,
    first_gain,
    first_shift,
    second_gain,
    second_shift,
    cotangent,
):
    row = lax.axis_index("row")
    col = lax.axis_index("col")
    member = 2 * (row % 2) + col % 2
    last = member == 3

    small = (
        mixer_bias,
        merge_bias,
        expand_bias,
        reduce_bias,
        first_gain,
        first_shift,
        second_gain,
        second_shift,
    )
    widths = [values.shape[1] for values in small]
    starts = [sum(widths[:at]) for at in range(len(widths))]
    packed = jnp.concatenate(small, axis=1).astype(bf16)
    gathered = lax.all_gather(packed, BLOCKS)
    gathered = gathered.reshape(4, 4, 3, -1).transpose(0, 2, 1, 3).reshape(12, 4, -1).astype(f32)
    vectors = [
        gathered[:, :, start : start + width].reshape(12, 4 * width)
        for start, width in zip(starts, widths)
    ]
    pairs = vectors[0].reshape(12, 2, HD)
    mixed_bias = jnp.stack([pairs[:, 0], jnp.zeros_like(pairs[:, 0]), pairs[:, 1]], axis=1)
    mixed_bias = widen(mixed_bias.reshape(4, 1, 9 * HD))
    merge_vec, expand_vec, reduce_vec, gain_one, shift_one, gain_two, shift_two = [
        values.reshape(-1) for values in vectors[1:]
    ]

    mixer = lax.all_gather(widen(mixer_weight.astype(bf16)), BLOCKS).reshape(4, D, WIDE)
    merge = lax.all_gather(merge_weight.astype(bf16), BLOCKS).reshape(4, 3 * HD, D)
    merge = jnp.concatenate(
        [merge[:, : 2 * HD], jnp.zeros((4, HD, D), bf16), merge[:, 2 * HD :]], axis=1
    )
    expand = lax.all_gather(expand_weight.astype(bf16), BLOCKS).reshape(4, D, D)
    reduce = lax.all_gather(reduce_weight.astype(bf16), BLOCKS).reshape(4, D, D)

    rows = to_members(inputs, col, member).astype(f32)
    cotan = to_members(cotangent, col, member)
    cotan_wide = cotan.astype(f32)

    normed_one, scaled_one, inverse_one = norm(rows, gain_one, shift_one)
    normed_one = normed_one.astype(bf16)
    mixed = (many(mixer, normed_one, (1,), (1,)).transpose(0, 2, 1) + mixed_bias).astype(bf16)
    slots = to_slots(mixed.reshape(4, 3, ROWS, WIDE), last).reshape(3, KEYS, WIDE)
    outs, sums = attend(slots)
    heads = from_slots(outs.reshape(3, 4, ROWS, 256), last).reshape(4, 3 * ROWS, 256)
    state = rows + many(heads, merge, (0, 2), (0, 1)) + merge_vec
    normed_two, scaled_two, inverse_two = norm(state, gain_two, shift_two)
    normed_two = normed_two.astype(bf16)
    hidden = many(expand, normed_two, (1,), (1,)).transpose(0, 2, 1) + expand_vec.reshape(4, 1, D)
    active, slope = gelu_parts(hidden)
    active = active.astype(bf16)
    result = state + many(active, reduce, (0, 2), (0, 1)) + reduce_vec
    outputs = from_members(result.astype(bf16), col, member)

    grad_reduce_mat = many(active, cotan, (1,), (0,))
    grad_reduce_vec = jnp.sum(cotan_wide, axis=0)
    grad_active = many(reduce, cotan, (2,), (1,)).transpose(0, 2, 1)
    grad_hidden = (grad_active * slope).astype(bf16)
    grad_expand_mat = many(normed_two, grad_hidden, (0,), (1,)).transpose(1, 0, 2)
    grad_expand_vec = jnp.sum(grad_hidden.astype(f32), axis=1)
    back_two, grad_gain_two, grad_shift_two = norm_back(
        many(grad_hidden, expand, (0, 2), (0, 2)), scaled_two, inverse_two, gain_two
    )
    grad_state = cotan_wide + back_two
    grad_branch = grad_state.astype(bf16)
    grad_merge_mat = many(heads, grad_branch, (1,), (0,))
    grad_merge_vec = jnp.sum(grad_branch.astype(f32), axis=0)
    grad_heads = many(merge, grad_branch, (2,), (1,)).transpose(0, 2, 1).astype(bf16)
    grad_slots = to_slots(grad_heads.reshape(4, 3, ROWS, 256), last).reshape(3, KEYS, 256)
    mixed_slots = attend_back(slots, grad_slots, sums)
    grad_mixed = from_slots(mixed_slots.reshape(3, 4, ROWS, WIDE), last)
    grad_mixed = grad_mixed.reshape(4, 3 * ROWS, WIDE)
    grad_mixer_mat = many(normed_one, grad_mixed, (0,), (1,)).transpose(1, 0, 2)
    bias_sums = narrow(jnp.sum(grad_mixed.astype(f32), axis=1)).reshape(12, 3, HD)
    grad_mixer_vec = jnp.stack([bias_sums[:, 0], bias_sums[:, 2]], axis=1)
    back_one, grad_gain_one, grad_shift_one = norm_back(
        many(grad_mixed, mixer, (0, 2), (0, 2)), scaled_one, inverse_one, gain_one
    )
    input_grad = from_members((grad_state + back_one).astype(bf16), col, member).astype(f32)

    def scatter(values):
        blocks = values.astype(bf16).reshape(16, -1, values.shape[-1])
        return lax.psum_scatter(blocks, BLOCKS, scatter_dimension=0, tiled=False)

    grad_merge_mat = jnp.concatenate(
        [grad_merge_mat[:, : 2 * HD], grad_merge_mat[:, 3 * HD :]], axis=1
    )
    parts = [
        scatter(grad_reduce_mat),
        scatter(grad_expand_mat),
        scatter(grad_merge_mat),
        scatter(grad_mixer_mat),
    ]
    part_reduce, part_expand, part_merge, part_mixer = [
        lax.psum(part.astype(f32), "dp") for part in parts
    ]
    totals = (
        grad_mixer_vec,
        grad_merge_vec,
        grad_expand_vec,
        grad_reduce_vec,
        grad_gain_one,
        grad_shift_one,
        grad_gain_two,
        grad_shift_two,
    )
    sizes = [values.size for values in totals]
    joined = lax.psum(
        jnp.concatenate([values.reshape(-1) for values in totals]), ("dp", "row", "col")
    )
    shares = []
    for at, width in enumerate(widths):
        start = sum(sizes[:at])
        whole = joined[start : start + sizes[at]].reshape(12, 4 * width)
        shares.append(lax.dynamic_slice(whole, (3 * col, width * row), (3, width)))
    return (
        outputs,
        input_grad,
        narrow(part_mixer),
        shares[0],
        part_merge,
        shares[1],
        part_expand,
        shares[2],
        part_reduce,
        shares[3],
        shares[4],
        shares[5],
        shares[6],
        shares[7],
    )


def solution(mesh):
    rows = P(("dp", "row"), "col", None)
    square = P("row", "col")
    flat = P(("col", "row"), None)
    small = P("col", "row")
    weights = (square, small, flat, small, square, small, flat, small, small, small, small, small)
    return jax.shard_map(
        body,
        mesh=mesh,
        in_specs=(rows,) + weights + (rows,),
        out_specs=(rows, rows) + weights,
        check_vma=False,
    )
```

time: 1920 us -> 754 us (0.39)
  waiting for transfers between devices: 1200 us -> 120 us
  matrix products: 251 us -> 91.2 us
  Pallas kernels: 0 us -> 83.3 us
  blocking collectives: 175 us -> 103 us
  starting transfers between devices: 1.72 us -> 72.6 us
    reduce_scatter x8 -> x4, waiting for transfers between devices: 695 us -> 0.01 us  [scatter(): return lax.psum_scatter(blocks, BLOCKS, scatter_dimension=0, tiled=False)]
    all_gather x6 -> x4, waiting for transfers between devices: 376 us -> 0.04 us  [the longest x1 0.02 us: body(): expand = lax.all_gather(expand_weight.astype(bf16), BLOCKS).reshape(4, D, D)]
    dot_general x75 -> x12, matrix products: 251 us -> 91.2 us  [many(): lax.dot_general(left, right, ((left_dims, right_dims), (left_batch, right...]
    unnamed x31 -> x9, waiting for transfers between devices: 125 us -> 0.15 us
    ppermute x0 -> x28, waiting for transfers between devices: none -> 119 us  [the longest x6 45.4 us: to_slots(): lax.ppermute(jnp.where(last, values[:3, at], values[3]), PLANE, swap_pair...]
    pallas_call x0 -> x2, Pallas kernels: none -> 83.3 us  [the longest x1 55.5 us: attend_back(): pl.pallas_call(attend_back_kernel, grid=(slots,), in_specs=[pl.BlockSpec(...]
    ppermute x0 -> x28, starting transfers between devices: none -> 72.3 us  [the longest x8 34.5 us: to_members(): lax.ppermute(take(blocks, col ^ step), PLANE, spread_pairs(step))]
    psum x7 -> x1, blocking collectives: 117 us -> 50.2 us  [body(): lax.psum(jnp.concatenate([values.reshape(-1) for values in totals]), ('dp...]
  transfers between devices with their start and end apart: 23 -> 37, of which waited for: 20 -> 7; matrix products, arithmetic and copies ran while one was open for 8% -> 42% of each run, Pallas kernels for 0% -> 11%
where the time goes in v1:
time: 754 us; the launch traced here: 739 us
  local copies, waits for them, and re-layouts  181 us (24%)
  waiting for transfers between devices  120 us (16%)
  blocking collectives  103 us (14%)
  matrix products  91.2 us (12%)
  Pallas kernels  83.3 us (11%)
  other arithmetic  72.7 us (10%)
  starting transfers between devices  72.6 us (10%)
  between operations  15.4 us (2%)
    dot_general x12, matrix products, many(): lax.dot_general(left, right, ((left_dims, right_dims), (left_batch, right...  91.2 us
    pallas_call x1, Pallas kernels, attend_back(): pl.pallas_call(attend_back_kernel, grid=(slots,), in_specs=[pl.BlockSpec(...  55.5 us
    all_gather x1, blocking collectives, body(): gathered = lax.all_gather(packed, BLOCKS)  53.2 us
    psum x1, blocking collectives, body(): lax.psum(jnp.concatenate([values.reshape(-1) for values in totals]), ('dp...  50.2 us
    ppermute x6, waiting for transfers between devices, to_slots(): lax.ppermute(jnp.where(last, values[:3, at], values[3]), PLANE, swap_pair...  45.4 us
    ppermute x8, waiting for transfers between devices, from_members(): lax.ppermute(take(parts, member ^ step), PLANE, [(target, source) for sou...  37.4 us
    ppermute x6, waiting for transfers between devices, from_slots(): lax.ppermute(jnp.where(last, values[at, :3], values[:, 3]), PLANE, swap_p...  36.5 us
    unnamed x138, local copies, waits for them, and re-layouts  35.1 us
  transfers between devices with their start and end apart: 37, of which 7 were waited for; matrix products, arithmetic and copies ran while one was open for 42% of the time, Pallas kernels for 11%

profile of v1, /device:TPU:0, one launch (start us, length us, event | category | flops | bytes accessed | tf_op | source)
XLA Modules:
  0.0 739.4 jit_solution(8539995918278728190)
XLA Ops:
  12.1 7.7 %copy.126 = bf16[1821,3,128]{2,1,0:T(4,128)(2,1)S(1)} copy(bf16[1821,3,128]{2,0,1:T(8,128)(2,1)S(1)} %copy-done.15) | data formatting | bytes 2797056 | tf_op args[0]
  31.3 53.2 %all_gather.30 = bf16[16,3,192]{2,1,0:T(4,128)(2,1)S(1)} all-gather(bf16[1,3,192]{2,1,0:T(4,128)(2,1)S(1)} %concatenate.104), channel_id=1, replica_groups=mesh['dp'=2,'row'=4,'col'=4] {'col','row'}, dimensions={0}, use_global_device_ids=true | all-gather | bytes 19584 | tf_op jit(solution)/shard_map/all_gather | solution.py:331
  107.6 7.9 %copy.133 = bf16[3,2,152,12,64]{2,1,0,4,3:T(2,128)(2,1)} copy(bf16[3,2,152,12,64]{4,1,3,2,0:T(2,128)(2,1)S(1)} %add_convert_fusion.1) | data formatting | bytes 2801664 | tf_op jit(solution)/shard_map/convert_element_type | solution.py:357
  134.2 9.0 %collective-permute-start.4 = (bf16[3,304,640]{2,1,0:T(8,128)(2,1)}, bf16[3,304,640]{2,1,0:T(8,128)(2,1)}, u32[]{:S(2)}, u32[]{:S(2)}) collective-permute-start(bf16[3,304,640]{2,1,0:T(8,128)(2,1)} %get-tuple-element.90), channel_id=1, source_target_pairs={{0,5},{5,0},{2,7},{7,2},{8,13},{13,8},{10,15},{15,10},{16,21},{21,... | collective-permute-start | bytes 3502088 | tf_op jit(solution)/shard_map/ppermute | solution.py:245
  143.2 7.7 %copy.143 = bf16[1821,3,128]{2,1,0:T(4,128)(2,1)S(1)} copy(bf16[1821,3,128]{2,0,1:T(8,128)(2,1)S(1)} %copy-done.16) | data formatting | bytes 2797056 | tf_op args[13]
  163.3 22.4 %collective-permute-start.17 = (bf16[456,384]{1,0:T(8,128)(2,1)S(1)}, bf16[456,384]{1,0:T(8,128)(2,1)}, u32[]{:S(2)}, u32[]{:S(2)}) collective-permute-start(bf16[456,384]{1,0:T(8,128)(2,1)S(1)} %get-tuple-element.115), channel_id=1, source_target_pairs={{0,5},{1,4},{2,1},{3,0},{4,7},{5,6},{6,3},{7,2},{8,13},{9,12},{10,... | collective-permute-start | bytes 1050632 | tf_op jit(solution)/shard_map/ppermute | solution.py:201
  185.8 33.1 %collective-permute-done.4 = bf16[3,304,640]{2,1,0:T(8,128)(2,1)} collective-permute-done((bf16[3,304,640]{2,1,0:T(8,128)(2,1)}, bf16[3,304,640]{2,1,0:T(8,128)(2,1)}, u32[]{:S(2)}, u32[]{:S(2)}) %collective-permute-start.4) | collective-permute-done | bytes 1167392 | tf_op jit(solution)/shard_map/ppermute | solution.py:245
  226.5 27.7 %attend.1 = (bf16[3,1216,256]{2,1,0:T(8,128)(2,1)}, f32[3,1216,128]{2,1,0:T(8,128)}) custom-call(bf16[3,1216,640]{2,1,0:T(8,128)(2,1)} %bitcast.373), custom_call_target="tpu_custom_call" | custom-call | flops 6813646848 | bytes 8404992 | tf_op jit(solution)/shard_map/attend/pallas_call | solution.py:92
  270.5 7.9 %copy.144 = bf16[3,2,152,12,64]{2,1,0,4,3:T(2,128)(2,1)} copy(bf16[3,2,152,12,64]{4,1,3,2,0:T(2,128)(2,1)S(1)} %bitcast.348) | data formatting | bytes 2801664 | tf_op jit(solution)/shard_map/transpose | solution.py:207
  310.4 11.1 %fusion.9 = (bf16[4,912,768]{2,1,0:T(8,128)(2,1)}, f32[912,4,768]{2,0,1:T(8,128)}) fusion(f32[4,768]{1,0:T(4,128)S(1)} %add.269, bf16[4,768,768]{2,1,0:T(8,128)(2,1)} %bitcast.418, f32[912,768]{1,0:T(8,128)} %copy-done.9, f32[768]{0:T(1024)S(1)} %add.266, f32[768]{0:T(1024)S(1)} %mul.177, f32[912]{0:T(1024)S(1)} %add_rsqrt_fusion.1, ...), kind=kOutput, calls=%fused_computation.12 | convolution fusion | flops 4323667968 | bytes 24355968 | tf_op jit(solution)/shard_map/dot_general | solution.py:283
  321.5 12.2 %convert_reduce_fusion = (f32[4,768]{1,0:T(4,128)S(1)}, bf16[4,912,768]{2,1,0:T(8,128)(2,1)S(1)}) fusion(f32[912,4,768]{2,0,1:T(8,128)} %get-tuple-element.179, f32[4,768]{1,0:T(4,128)S(1)} %add.269, bf16[4,768,768]{2,1,0:T(8,128)(2,1)} %bitcast.416, bf16[912,768]{0,1:T(8,128)(2,1)} %reshape.476), kind=kOutput, calls=%fused_computation.13 | convolution fusion | flops 4339774464 | bytes 22953984 | tf_op jit(solution)/shard_map/dot_general | solution.py:283
  344.5 10.0 %convolution_convert_fusion.1 = bf16[768,4,768]{2,0,1:T(8,128)(2,1)} fusion(bf16[4,912,768]{2,1,0:T(8,128)(2,1)} %copy-done.56, f32[912,768]{1,0:T(8,128)} %copy-done.9, f32[768]{0:T(1024)S(1)} %add.266, f32[768]{0:T(1024)S(1)} %mul.177, f32[912]{0:T(1024)S(1)} %add_rsqrt_fusion.1, f32[912]{0:T(1024)S(1)} %broadcast_multiply_fusion.5), kind=kOutput, calls=%fused_computation.25 | convolution fusion | flops 4309217280 | bytes 13137024 | tf_op jit(solution)/shard_map/dot_general | solution.py:283
  354.6 9.4 %convolution_convert_fusion = bf16[4,768,768]{2,1,0:T(8,128)(2,1)} fusion(bf16[4,912,768]{2,1,0:T(8,128)(2,1)} %get-tuple-element.178, bf16[912,768]{0,1:T(8,128)(2,1)} %reshape.476), kind=kOutput, calls=%fused_computation.24 | convolution fusion | flops 4305715200 | bytes 11722752 | tf_op jit(solution)/shard_map/dot_general | solution.py:283
  375.4 12.3 %collective-permute-done.18 = bf16[3,304,256]{2,1,0:T(8,128)(2,1)S(1)} collective-permute-done((bf16[3,304,256]{2,1,0:T(8,128)(2,1)S(1)}, bf16[3,304,256]{2,1,0:T(8,128)(2,1)S(1)}, u32[]{:S(2)}, u32[]{:S(2)}) %collective-permute-start.18) | collective-permute-done | bytes 466976 | tf_op jit(solution)/shard_map/ppermute | solution.py:245
  389.5 55.5 %attend_back.1 = bf16[3,1216,640]{2,1,0:T(8,128)(2,1)} custom-call(bf16[3,1216,640]{2,1,0:T(8,128)(2,1)} %bitcast.374, bf16[3,1216,256]{2,1,0:T(8,128)(2,1)} %bitcast.384, f32[3,1216,128]{2,1,0:T(8,128)} %get-tuple-element.17.sum_ref), custom_call_target="tpu_custom_call" | custom-call | flops 17034117120 | bytes 13074432 | tf_op jit(solution)/shard_map/attend_back/pallas_call | solution.py:152
  456.9 36.5 %collective-permute-done.21 = bf16[3,304,640]{2,1,0:T(8,128)(2,1)} collective-permute-done((bf16[3,304,640]{2,1,0:T(8,128)(2,1)}, bf16[3,304,640]{2,1,0:T(8,128)(2,1)}, u32[]{:S(2)}, u32[]{:S(2)}) %collective-permute-start.21) | collective-permute-done | bytes 1167392 | tf_op jit(solution)/shard_map/ppermute | solution.py:256
  506.1 11.1 %fusion.13 = bf16[912,768]{1,0:T(8,128)(2,1)} fusion(f32[912,768]{1,0:T(8,128)} %copy-done.9, bf16[4,912,768]{2,1,0:T(8,128)(2,1)} %get-tuple-element.178, bf16[4,768,768]{2,1,0:T(8,128)(2,1)} %bitcast.417, f32[768]{0:T(1024)S(1)} %add.276), kind=kOutput, calls=%fused_computation.36 | convolution fusion | flops 4305457152 | bytes 14527488 | tf_op jit(solution)/shard_map/dot_general | solution.py:283
  520.2 7.0 reshape.470
  527.3 12.3 %copy.142 = bf16[3,152,12,2,64]{4,3,2,1,0:T(2,128)(2,1)} copy(bf16[3,152,12,2,64]{1,3,0,4,2:T(2,128)(2,1)} %bitcast.361) | data formatting | bytes 2801664 | tf_op jit(solution)/shard_map/transpose | solution.py:215
  558.4 22.2 %collective-permute-done.11 = bf16[456,384]{1,0:T(8,128)(2,1)} collective-permute-done((bf16[456,384]{1,0:T(8,128)(2,1)}, bf16[456,384]{1,0:T(8,128)(2,1)}, u32[]{:S(2)}, u32[]{:S(2)}) %collective-permute-start.11) | collective-permute-done | bytes 350240 | tf_op jit(solution)/shard_map/ppermute | solution.py:219
  600.1 10.1 %fusion.10 = (f32[768]{0:T(1024)S(1)}, f32[912]{0:T(1024)}, f32[912]{0:T(1024)}, f32[768]{0:T(1024)S(1)}, f32[912,768,1]{1,0,2:T(8,128)}) fusion(f32[912,768]{1,0:T(8,128)} %reshape.525, f32[912]{0:T(1024)} %copy-done.39, f32[912]{0:T(1024)} %copy-done.41, f32[768]{0:T(1024)S(1)} %mul.198, bf16[4,768,640]{2,1,0:T(8,128)(2,1)} %bitcast.421, ...), kind=kOutput, calls=%fused_computation.29 | convolution fusion | flops 3594764800 | bytes 14228736 | tf_op jit(solution)/shard_map/dot_general | solution.py:283
  610.3 50.2 %psum.36 = f32[9216]{0:T(1024)S(1)} all-reduce(f32[9216]{0:T(1024)S(1)} %constant_dynamic-update-slice_fusion), channel_id=1, replica_groups=mesh['dp'=2,'row'=4,'col'=4] {'dp','row','col'}, use_global_device_ids=true, to_apply=%region_18.19 | all-reduce | flops 9216 | bytes 73728 | tf_op jit(solution)/shard_map/psum | solution.py:424
  681.2 8.1 %copy.154 = bf16[3,152,12,2,64]{4,3,2,1,0:T(2,128)(2,1)} copy(bf16[3,152,12,2,64]{1,3,0,4,2:T(2,128)(2,1)S(1)} %bitcast.362) | data formatting | bytes 2801664 | tf_op jit(solution)/shard_map/transpose | solution.py:215
  705.6 10.8 %collective-permute-done.25 = bf16[456,384]{1,0:T(8,128)(2,1)S(1)} collective-permute-done((bf16[456,384]{1,0:T(8,128)(2,1)S(1)}, bf16[456,384]{1,0:T(8,128)(2,1)S(1)}, u32[]{:S(2)}, u32[]{:S(2)}) %collective-permute-start.25) | collective-permute-done | bytes 350240 | tf_op jit(solution)/shard_map/ppermute | solution.py:219
  (373 shorter events, 268.2 us)
Async XLA Ops:
  7.2 113.4 %all-gather.9.cloned.1.call-start = ((), (), s32[]{:S(2)}) async-start(), calls=%async_computation.8 | async-start | bytes 4177920 | tf_op jit(solution)/shard_map/all_gather | solution.py:344
  9.6 290.6 %all-gather.11.cloned.1.call-start = ((), (), s32[]{:S(2)}) async-start(), calls=%async_computation.9 | async-start | bytes 1253376 | tf_op jit(solution)/shard_map/all_gather | solution.py:345
  11.2 299.2 %all-gather.13.cloned.1.call-start = ((), (), s32[]{:S(2)}) async-start(), calls=%async_computation.10 | async-start | bytes 5013504 | tf_op jit(solution)/shard_map/all_gather | solution.py:349
  12.0 309.5 %all-gather.15.cloned.1.call-start = ((), (), s32[]{:S(2)}) async-start(), calls=%async_computation.11 | async-start | bytes 5013504 | tf_op jit(solution)/shard_map/all_gather | solution.py:350
  22.7 65.1 %collective-permute-start = (bf16[456,384]{1,0:T(8,128)(2,1)}, bf16[456,384]{1,0:T(8,128)(2,1)S(1)}, u32[]{:S(2)}, u32[]{:S(2)}) collective-permute-start(bf16[456,384]{1,0:T(8,128)(2,1)} %get-tuple-element.128), channel_id=1, source_target_pairs={{0,0},{1,1},{2,4},{3,5},{4,2},{5,3},{6,6},{7,7},{8,8},{9,9},{10,12... | collective-permute-start | bytes 1050632 | tf_op jit(solution)/shard_map/ppermute | solution.py:201
  24.4 63.5 %collective-permute-start.1 = (bf16[456,384]{1,0:T(8,128)(2,1)S(1)}, bf16[456,384]{1,0:T(8,128)(2,1)S(1)}, u32[]{:S(2)}, u32[]{:S(2)}) collective-permute-start(bf16[456,384]{1,0:T(8,128)(2,1)S(1)} %get-tuple-element.129), channel_id=1, source_target_pairs={{0,1},{1,0},{2,5},{3,4},{4,3},{5,2},{6,7},{7,6},{8,9},{9,8},{10,13... | collective-permute-start | bytes 1050632 | tf_op jit(solution)/shard_map/ppermute | solution.py:201
  27.4 60.4 %collective-permute-start.2 = (bf16[456,384]{1,0:T(8,128)(2,1)S(1)}, bf16[456,384]{1,0:T(8,128)(2,1)S(1)}, u32[]{:S(2)}, u32[]{:S(2)}) collective-permute-start(bf16[456,384]{1,0:T(8,128)(2,1)S(1)} %get-tuple-element.130), channel_id=1, source_target_pairs={{0,4},{1,5},{2,0},{3,1},{4,6},{5,7},{6,2},{7,3},{8,12},{9,13},{10,... | collective-permute-start | bytes 1050632 | tf_op jit(solution)/shard_map/ppermute | solution.py:201
  29.9 57.9 %collective-permute-start.3 = (bf16[456,384]{1,0:T(8,128)(2,1)S(1)}, bf16[456,384]{1,0:T(8,128)(2,1)S(1)}, u32[]{:S(2)}, u32[]{:S(2)}) collective-permute-start(bf16[456,384]{1,0:T(8,128)(2,1)S(1)} %get-tuple-element.131), channel_id=1, source_target_pairs={{0,5},{1,4},{2,1},{3,0},{4,7},{5,6},{6,3},{7,2},{8,13},{9,12},{10,... | collective-permute-start | bytes 1050632 | tf_op jit(solution)/shard_map/ppermute | solution.py:201
  31.0 630.2 %reduce-scatter.7.cloned.1.call-start = ((), (), s32[]{:S(2)}) async-start(), calls=%async_computation.5 | async-start | bytes 1253376 | tf_op jit(solution)/shard_map/reduce_scatter | solution.py:399
  130.9 29.5 %collective-permute-start.5 = (bf16[3,304,640]{2,1,0:T(8,128)(2,1)}, bf16[3,304,640]{2,1,0:T(8,128)(2,1)}, u32[]{:S(2)}, u32[]{:S(2)}) collective-permute-start(bf16[3,304,640]{2,1,0:T(8,128)(2,1)} %get-tuple-element.88), channel_id=1, source_target_pairs={{1,5},{5,1},{3,7},{7,3},{9,13},{13,9},{11,15},{15,11},{17,21},{21,... | collective-permute-start | bytes 3502088 | tf_op jit(solution)/shard_map/ppermute | solution.py:245
  132.5 30.8 %collective-permute-start.6 = (bf16[3,304,640]{2,1,0:T(8,128)(2,1)}, bf16[3,304,640]{2,1,0:T(8,128)(2,1)}, u32[]{:S(2)}, u32[]{:S(2)}) collective-permute-start(bf16[3,304,640]{2,1,0:T(8,128)(2,1)} %get-tuple-element.89), channel_id=1, source_target_pairs={{4,5},{5,4},{6,7},{7,6},{12,13},{13,12},{14,15},{15,14},{20,21},{2... | collective-permute-start | bytes 3502088 | tf_op jit(solution)/shard_map/ppermute | solution.py:245
  134.2 84.6 %collective-permute-start.4 = (bf16[3,304,640]{2,1,0:T(8,128)(2,1)}, bf16[3,304,640]{2,1,0:T(8,128)(2,1)}, u32[]{:S(2)}, u32[]{:S(2)}) collective-permute-start(bf16[3,304,640]{2,1,0:T(8,128)(2,1)} %get-tuple-element.90), channel_id=1, source_target_pairs={{0,5},{5,0},{2,7},{7,2},{8,13},{13,8},{10,15},{15,10},{16,21},{21,... | collective-permute-start | bytes 3502088 | tf_op jit(solution)/shard_map/ppermute | solution.py:245
  156.0 102.2 %collective-permute-start.14 = (bf16[456,384]{1,0:T(8,128)(2,1)}, bf16[456,384]{1,0:T(8,128)(2,1)S(1)}, u32[]{:S(2)}, u32[]{:S(2)}) collective-permute-start(bf16[456,384]{1,0:T(8,128)(2,1)} %get-tuple-element.112), channel_id=1, source_target_pairs={{0,0},{1,1},{2,4},{3,5},{4,2},{5,3},{6,6},{7,7},{8,8},{9,9},{10,12... | collective-permute-start | bytes 1050632 | tf_op jit(solution)/shard_map/ppermute | solution.py:201
  157.6 102.0 %collective-permute-start.15 = (bf16[456,384]{1,0:T(8,128)(2,1)S(1)}, bf16[456,384]{1,0:T(8,128)(2,1)S(1)}, u32[]{:S(2)}, u32[]{:S(2)}) collective-permute-start(bf16[456,384]{1,0:T(8,128)(2,1)S(1)} %get-tuple-element.113), channel_id=1, source_target_pairs={{0,1},{1,0},{2,5},{3,4},{4,3},{5,2},{6,7},{7,6},{8,9},{9,8},{10,13... | collective-permute-start | bytes 1050632 | tf_op jit(solution)/shard_map/ppermute | solution.py:201
  160.4 101.6 %collective-permute-start.16 = (bf16[456,384]{1,0:T(8,128)(2,1)S(1)}, bf16[456,384]{1,0:T(8,128)(2,1)}, u32[]{:S(2)}, u32[]{:S(2)}) collective-permute-start(bf16[456,384]{1,0:T(8,128)(2,1)S(1)} %get-tuple-element.114), channel_id=1, source_target_pairs={{0,4},{1,5},{2,0},{3,1},{4,6},{5,7},{6,2},{7,3},{8,12},{9,13},{10,... | collective-permute-start | bytes 1050632 | tf_op jit(solution)/shard_map/ppermute | solution.py:201
  163.3 98.7 %collective-permute-start.17 = (bf16[456,384]{1,0:T(8,128)(2,1)S(1)}, bf16[456,384]{1,0:T(8,128)(2,1)}, u32[]{:S(2)}, u32[]{:S(2)}) collective-permute-start(bf16[456,384]{1,0:T(8,128)(2,1)S(1)} %get-tuple-element.115), channel_id=1, source_target_pairs={{0,5},{1,4},{2,1},{3,0},{4,7},{5,6},{6,3},{7,2},{8,13},{9,12},{10,... | collective-permute-start | bytes 1050632 | tf_op jit(solution)/shard_map/ppermute | solution.py:201
  256.8 45.8 %collective-permute-start.8 = (bf16[3,304,256]{2,1,0:T(8,128)(2,1)}, bf16[3,304,256]{2,1,0:T(8,128)(2,1)}, u32[]{:S(2)}, u32[]{:S(2)}) collective-permute-start(bf16[3,304,256]{2,1,0:T(8,128)(2,1)} %get-tuple-element.97), channel_id=1, source_target_pairs={{1,5},{5,1},{3,7},{7,3},{9,13},{13,9},{11,15},{15,11},{17,21},{21,... | collective-permute-start | bytes 1400840 | tf_op jit(solution)/shard_map/ppermute | solution.py:256
  258.2 44.4 %collective-permute-start.9 = (bf16[3,304,256]{2,1,0:T(8,128)(2,1)}, bf16[3,304,256]{2,1,0:T(8,128)(2,1)}, u32[]{:S(2)}, u32[]{:S(2)}) collective-permute-start(bf16[3,304,256]{2,1,0:T(8,128)(2,1)} %get-tuple-element.98), channel_id=1, source_target_pairs={{4,5},{5,4},{6,7},{7,6},{12,13},{13,12},{14,15},{15,14},{20,21},{2... | collective-permute-start | bytes 1400840 | tf_op jit(solution)/shard_map/ppermute | solution.py:256
  259.7 43.0 %collective-permute-start.7 = (bf16[3,304,256]{2,1,0:T(8,128)(2,1)}, bf16[3,304,256]{2,1,0:T(8,128)(2,1)}, u32[]{:S(2)}, u32[]{:S(2)}) collective-permute-start(bf16[3,304,256]{2,1,0:T(8,128)(2,1)} %get-tuple-element.99), channel_id=1, source_target_pairs={{0,5},{5,0},{2,7},{7,2},{8,13},{13,8},{10,15},{15,10},{16,21},{21,... | collective-permute-start | bytes 1400840 | tf_op jit(solution)/shard_map/ppermute | solution.py:256
  344.4 318.3 %reduce-scatter.9.cloned.1.call-start = ((), (), s32[]{:S(2)}) async-start(), calls=%async_computation.6 | async-start | bytes 5013504 | tf_op jit(solution)/shard_map/reduce_scatter | solution.py:399
  354.5 310.0 %reduce-scatter.11.cloned.1.call-start = ((), (), s32[]{:S(2)}) async-start(), calls=%async_computation.7 | async-start | bytes 5013504 | tf_op jit(solution)/shard_map/reduce_scatter | solution.py:399
  364.0 302.4 %reduce-scatter.5.cloned.1.call-start = ((), (), s32[]{:S(2)}) async-start(), calls=%async_computation.4 | async-start | bytes 4177920 | tf_op jit(solution)/shard_map/reduce_scatter | solution.py:399
  452.7 40.6 %collective-permute-start.21 = (bf16[3,304,640]{2,1,0:T(8,128)(2,1)}, bf16[3,304,640]{2,1,0:T(8,128)(2,1)}, u32[]{:S(2)}, u32[]{:S(2)}) collective-permute-start(bf16[3,304,640]{2,1,0:T(8,128)(2,1)} %get-tuple-element.93), channel_id=1, source_target_pairs={{0,5},{5,0},{2,7},{7,2},{8,13},{13,8},{10,15},{15,10},{16,21},{21,... | collective-permute-start | bytes 3502088 | tf_op jit(solution)/shard_map/ppermute | solution.py:256
  506.1 220.8 %all-reduce.5.cloned.1.call-start = ((), (), s32[]{:S(2)}) async-start(), calls=%async_computation.12 | async-start | bytes 3637248 | tf_op jit(solution)/shard_map/psum | solution.py:411
  (72 other events, 916.8 us)
Sparse Core Ops, SparseCore 0:
  10.9 66.1 all-gather.8
  79.9 36.9 all-gather.10
  119.2 64.2 all-gather.12
  185.6 59.5 all-gather.14
  344.6 56.4 reduce-scatter.6
  404.8 85.6 reduce-scatter.8
  494.4 91.1 reduce-scatter.10
  589.4 72.4 reduce-scatter.4
  668.3 56.4 all-reduce.4
